TPU v7x, 128 devices: a whole 4x4x4 slice. The times are simulated.
128 devices in a mesh: gx: 16 (over z_hi, y, core), gy: 8 (over z_lo, x).
Axes of the slice: x: 4, y: 4, z: 4 (z_hi: 2, z_lo: 2; z = z_hi * 2 + z_lo), core: 2. Of those that a mesh axis runs over, the one named last changes fastest.
Arguments:
- slide_tokens: bfloat16 [128, 1024, 768], P('gy', 'gx'), may hold values from -9 to 9
- tissue: int32 [128, 1024], P('gy', 'gx'), may hold values 0 or 1
- grad_tokens: bfloat16 [128, 1024, 768], P('gy', 'gx'), may hold values from -6 to 6
- w_qkv: bfloat16 [768, 2304], replicated, may hold values from -1 to 1
- w_out: bfloat16 [768, 768], replicated, may hold values from -0.21875 to 0.21875
Outputs:
- block_out: bfloat16 [128, 1024, 768], P('gy', 'gx')
- grad_in: bfloat16 [128, 1024, 768], P('gy', 'gx')
- grad_wqkv: float32 [768, 2304], replicated
- grad_wout: float32 [768, 768], replicated
All inputs are finite; a program needn't handle non-finite values. No bound on the sum of `tissue` on one device may be relied on, other than what follows from the above.
Results may differ from a plain program's by a relative error of at most 0.013.
Values may be sent and summed in bfloat16 or wider, within the bound.
No kernel may reach another device: no remote copies, remote signals or barrier semaphores. Data moves between devices by JAX's collectives and lax.ppermute only.
A program may use at most 256 MiB of HBM per device.

v0:
```python
import math
import jax
import jax.numpy as jnp
from jax import lax
from jax.sharding import PartitionSpec as P

HEADS = 24
WIN = 8
SHIFT = 4
epsilon = 1e-05


def shifted_2(block, axis, distance):
    devices = range(lax.axis_size(axis))
    route = [((i - distance) % len(devices), i) for i in devices]
    return lax.ppermute(block, axis, route)


def windows(tensor):
    row_count, col_count, feature_dim = tensor.shape
    tensor = tensor.reshape(row_count // WIN, WIN, col_count // WIN, WIN, feature_dim)
    return tensor.transpose(0, 2, 1, 3, 4).reshape(-1, WIN * WIN, feature_dim)


def unwindows(tensor, row_count, col_count):
    feature_dim = tensor.shape[-1]
    tensor = tensor.reshape(row_count // WIN, col_count // WIN, WIN, WIN, feature_dim)
    return tensor.transpose(0, 2, 1, 3, 4).reshape(row_count, col_count, feature_dim)


def split_heads(tensor):
    return tensor.reshape(tensor.shape[0], tensor.shape[1], HEADS, -1)


def attend(qkv_win, keep_win):
    model_dim = qkv_win.shape[-1] // 3
    queries = split_heads(qkv_win[..., :model_dim])
    keys_part = split_heads(qkv_win[..., model_dim : 2 * model_dim])
    values_part = split_heads(qkv_win[..., 2 * model_dim :])
    score_scale = 1.0 / math.sqrt(model_dim // HEADS)
    scores = (
        jnp.einsum("wqhd,wkhd->whqk", queries, keys_part, preferred_element_type=jnp.float32)
        * score_scale
    )
    win_tokens = qkv_win.shape[1]
    itself = jnp.eye(win_tokens, dtype=bool)
    allowed = jnp.logical_or(keep_win[:, None, None, :] > 0.5, itself[None, None])
    scores = jnp.where(allowed, scores, -1e30)
    maximum = jnp.max(scores, -1, keepdims=True)
    exponent = jnp.exp(scores - maximum)
    attn_probs = exponent / jnp.sum(exponent, -1, keepdims=True)
    weights_half = attn_probs.astype(jnp.bfloat16)
    mixed_out = jnp.einsum(
        "whqk,wkhd->wqhd", weights_half, values_part, preferred_element_type=jnp.float32
    ).astype(jnp.bfloat16)
    return (mixed_out.reshape(qkv_win.shape[0], win_tokens, model_dim), attn_probs)


def attend_back(qkv_win, attn_probs, grad_mixed):
    model_dim = qkv_win.shape[-1] // 3
    window_count, win_tokens = (qkv_win.shape[0], qkv_win.shape[1])
    queries = split_heads(qkv_win[..., :model_dim])
    keys_part = split_heads(qkv_win[..., model_dim : 2 * model_dim])
    values_part = split_heads(qkv_win[..., 2 * model_dim :])
    score_scale = 1.0 / math.sqrt(model_dim // HEADS)
    grad_heads = split_heads(grad_mixed)
    grad_prob = jnp.einsum(
        "wqhd,wkhd->whqk", grad_heads, values_part, preferred_element_type=jnp.float32
    )
    weights_half = attn_probs.astype(jnp.bfloat16)
    grad_value = jnp.einsum(
        "whqk,wqhd->wkhd", weights_half, grad_heads, preferred_element_type=jnp.float32
    ).astype(jnp.bfloat16)
    grad_score = (
        attn_probs * (grad_prob - jnp.sum(grad_prob * attn_probs, -1, keepdims=True)) * score_scale
    )
    score_half = grad_score.astype(jnp.bfloat16)
    grad_query = jnp.einsum(
        "whqk,wkhd->wqhd", score_half, keys_part, preferred_element_type=jnp.float32
    ).astype(jnp.bfloat16)
    grad_key = jnp.einsum(
        "whqk,wqhd->wkhd", score_half, queries, preferred_element_type=jnp.float32
    ).astype(jnp.bfloat16)
    shape_out = (window_count, win_tokens, model_dim)
    return jnp.concatenate(
        [grad_query.reshape(shape_out), grad_key.reshape(shape_out), grad_value.reshape(shape_out)],
        -1,
    )


def layer_region(shifted, keep_mask, grad_shift, owned_mask, w_qkv, w_out):
    row_count, col_count, model_dim = shifted.shape
    flat_in = shifted.reshape(-1, model_dim).astype(jnp.float32)
    centered = flat_in - jnp.mean(flat_in, -1, keepdims=True)
    inv_sigma = lax.rsqrt(jnp.mean(centered * centered, -1, keepdims=True) + epsilon)
    normed = centered * inv_sigma
    hidden = normed.astype(jnp.bfloat16)
    qkv = jnp.dot(hidden, w_qkv, preferred_element_type=jnp.float32).astype(jnp.bfloat16)
    qkv_win = windows(qkv.reshape(row_count, col_count, -1))
    keep_win = windows(keep_mask[..., None])[..., 0]
    mixed_out, attn_probs = attend(qkv_win, keep_win)
    mixed_flat = unwindows(mixed_out, row_count, col_count).reshape(-1, model_dim)
    output = jnp.dot(mixed_flat, w_out, preferred_element_type=jnp.float32).astype(jnp.bfloat16)
    grad_flat = grad_shift.reshape(-1, model_dim)
    grad_mixed = jnp.dot(grad_flat, w_out.T, preferred_element_type=jnp.float32).astype(
        jnp.bfloat16
    )
    grad_qkv = attend_back(
        qkv_win, attn_probs, windows(grad_mixed.reshape(row_count, col_count, model_dim))
    )
    grad_qkv = unwindows(grad_qkv, row_count, col_count).reshape(-1, 3 * model_dim)
    own_column = owned_mask.reshape(-1, 1).astype(jnp.bfloat16)
    contract = (((0,), (0,)), ((), ()))
    grad_wout = lax.dot_general(
        mixed_flat * own_column, grad_flat, contract, preferred_element_type=jnp.float32
    )
    grad_wqkv = lax.dot_general(
        hidden * own_column, grad_qkv, contract, preferred_element_type=jnp.float32
    )
    grad_hidden = jnp.dot(grad_qkv, w_qkv.T, preferred_element_type=jnp.float32)
    grad_shifted = inv_sigma * (
        grad_hidden
        - jnp.mean(grad_hidden, -1, keepdims=True)
        - normed * jnp.mean(grad_hidden * normed, -1, keepdims=True)
    )
    shape_out = (row_count, col_count, model_dim)
    return (
        output.reshape(shape_out),
        grad_shifted.astype(jnp.bfloat16).reshape(shape_out),
        grad_wqkv,
        grad_wout,
    )


def local(slide_tokens, tissue, grad_tokens, w_qkv, w_out):
    row_count, col_count, model_dim = slide_tokens.shape
    keep_mask = tissue.astype(jnp.bfloat16)
    from_below = shifted_2((slide_tokens[:SHIFT], keep_mask[:SHIFT], grad_tokens[:SHIFT]), "gy", -1)
    tall_x = jnp.concatenate([slide_tokens[SHIFT:], from_below[0]], 0)
    tall_k = jnp.concatenate([keep_mask[SHIFT:], from_below[1]], 0)
    tall_g = jnp.concatenate([grad_tokens[SHIFT:], from_below[2]], 0)
    from_right = shifted_2((tall_x[:, :SHIFT], tall_k[:, :SHIFT], tall_g[:, :SHIFT]), "gx", -1)
    shifted_x = jnp.concatenate([tall_x[:, SHIFT:], from_right[0]], 1)
    shifted_k = jnp.concatenate([tall_k[:, SHIFT:], from_right[1]], 1)
    shifted_g = jnp.concatenate([tall_g[:, SHIFT:], from_right[2]], 1)
    owned_mask = jnp.ones((row_count, col_count), jnp.float32)
    attn_shift, grad_shift, part_qkv, part_out = layer_region(
        shifted_x, shifted_k, shifted_g, owned_mask, w_qkv, w_out
    )
    edge = col_count - SHIFT
    from_left = shifted_2((attn_shift[:, edge:], grad_shift[:, edge:]), "gx", 1)
    wide_attn = jnp.concatenate([from_left[0], attn_shift[:, :edge]], 1)
    wide_grad = jnp.concatenate([from_left[1], grad_shift[:, :edge]], 1)
    bottom = row_count - SHIFT
    from_above = shifted_2((wide_attn[bottom:], wide_grad[bottom:]), "gy", 1)
    attn_tile = jnp.concatenate([from_above[0], wide_attn[:bottom]], 0)
    grad_tile = jnp.concatenate([from_above[1], wide_grad[:bottom]], 0)
    grad_wqkv, grad_wout = lax.psum((part_qkv, part_out), ("gx", "gy"))
    block_out = (slide_tokens.astype(jnp.float32) + attn_tile.astype(jnp.float32)).astype(
        jnp.bfloat16
    )
    grad_in = (grad_tokens.astype(jnp.float32) + grad_tile.astype(jnp.float32)).astype(jnp.bfloat16)
    return (block_out, grad_in, grad_wqkv, grad_wout)


def solution(mesh):
    placed = (P("gy", "gx", None), P("gy", "gx"), P("gy", "gx", None), P(), P())
    return jax.shard_map(
        local,
        mesh=mesh,
        in_specs=placed,
        out_specs=(P("gy", "gx", None), P("gy", "gx", None), P(), P()),
        check_vma=False,
    )
```

profile of v0, /device:TPU:1, one launch (start us, length us, event | category | flops | bytes accessed | tf_op | source)
XLA Modules:
  0.0 433.7 jit_solution(9250790033228147858)
XLA Ops:
  7.2 0.9 convert_element_type.101
  8.1 4.7 %collective-permute-start.2 = (bf16[4,64]{1,0:T(4,128)(2,1)S(1)}, bf16[4,64]{1,0:T(4,128)(2,1)S(1)}, u32[]{:S(2)}, u32[]{:S(2)}) collective-permute-start(bf16[4,64]{1,0:T(4,128)(2,1)S(1)} %slice.99), channel_id=1, source_target_pairs={{1,0},{2,1},{3,2},{4,3},{5,4},{6,5},{7,6},{0,7},{9,8},{10,9},{11,1... | collective-permute-start | bytes 1544 | tf_op jit(solution)/shard_map/ppermute | solution.py:16
  12.8 1.8 slice.88
  15.2 1.8 slice.73
  17.8 2.4 slice.72
  20.2 1.1 slice.87
  21.3 1.5 collective-permute-start.3
  22.9 2.8 collective-permute-done.3
  25.7 0.7 maximum_compare_fusion
  26.4 0.8 gt.22
  27.8 0.8 gt.24
  28.6 1.6 broadcast_or_fusion
  30.3 2.7 collective-permute-done
  32.9 1.0 pad_maximum_fusion.7
  33.9 1.9 collective-permute-start.1
  35.8 1.6 pad_maximum_fusion.6
  37.5 4.3 collective-permute-start.7
  41.7 1.4 slice_maximum_fusion.1
  43.2 2.8 slice_maximum_fusion
  47.3 0.7 div.23
  48.6 1.7 pad_maximum_fusion.3
  50.3 1.2 copy-done.18
  51.5 1.4 convolution_convert_fusion.1
  53.0 1.3 copy.38
  55.5 4.5 %convolution_convert_fusion = bf16[1024,2304]{1,0:T(8,128)(2,1)S(1)} fusion(bf16[1024,768]{1,0:T(8,128)(2,1)S(1)} %fusion.20, bf16[768,2304]{1,0:T(8,128)(2,1)S(1)} %copy-done), kind=kOutput, calls=%fused_computation.12 | convolution fusion | flops 3626237952 | bytes 9830400 | tf_op jit(solution)/shard_map/dot_general | solution.py:98
  60.5 2.3 fusion.40
  62.8 4.1 copy.18
  66.9 4.2 copy.17
  71.1 4.2 copy.15
  75.3 8.2 %reshape_reshape.22 = bf16[16,64,24,32]{3,2,1,0:T(8,128)(2,1)} reshape(bf16[2,8,8,8,768]{4,3,2,1,0:T(8,128)(2,1)} %bitcast.88) | data formatting | bytes 3145728 | tf_op jit(solution)/shard_map/reshape;reshape | solution.py:32
  83.5 7.0 %copy.23 = bf16[16,64,24,32]{1,3,2,0:T(8,128)(2,1)} copy(bf16[16,64,24,32]{3,2,1,0:T(8,128)(2,1)} %reshape_reshape.22) | data formatting | bytes 3145728 | tf_op jit(solution)/shard_map/reshape;reshape | solution.py:32
  90.5 9.2 %fusion.42 = f32[16,24,64,64]{2,3,1,0:T(8,128)} fusion(bf16[16,64,24,32]{1,3,2,0:T(8,128)(2,1)} %copy.23, bf16[16,64,24,32]{1,3,2,0:T(8,128)(2,1)} %bitcast.83), kind=kOutput, calls=%fused_computation.69 | convolution fusion | flops 100663296 | bytes 9437184 | tf_op jit(solution)/shard_map/wqhd,wkhd->whqk/dot_general | solution.py:67
  99.7 10.5 %fusion.41 = (f32[16,24,64]{2,1,0:T(8,128)}, f32[16,24,64,64]{2,3,1,0:T(8,128)}) fusion(pred[16,64,64]{1,2,0:T(8,128)(4,1)} %broadcast_or_fusion, bf16[16,64,24,32]{1,3,2,0:T(8,128)(2,1)} %bitcast.95, bf16[16,64,24,32]{1,3,2,0:T(8,128)(2,1)} %bitcast.93), kind=kOutput, calls=%fused_computation.68 | convolution fusion | flops 106954816 | bytes 9601024 | tf_op jit(solution)/shard_map/sub | solution.py:50
  110.2 19.8 %convert_bitcast_fusion.2 = bf16[16,64,24,32]{1,3,2,0:T(8,128)(2,1)} fusion(bf16[16,64,24,32]{1,3,2,0:T(8,128)(2,1)} %bitcast.94, f32[16,24,64,64]{2,3,1,0:T(8,128)} %fusion.42, f32[16,24,64,64]{2,3,1,0:T(8,128)} %get-tuple-element.12, f32[16,24,64]{2,1,0:T(8,128)} %get-tuple-element.11), kind=kOutput, calls=%fused_computation.24 | convolution fusion | flops 112484416 | bytes 15826944 | tf_op jit(solution)/shard_map/whqk,wkhd->wqhd/dot_general | solution.py:78
  130.0 20.0 %convert_bitcast_fusion.1 = bf16[16,64,24,32]{1,3,2,0:T(8,128)(2,1)} fusion(bf16[16,64,24,32]{1,3,2,0:T(8,128)(2,1)} %bitcast.96, f32[16,24,64,64]{2,3,1,0:T(8,128)} %fusion.42, f32[16,24,64,64]{2,3,1,0:T(8,128)} %get-tuple-element.12, f32[16,24,64]{2,1,0:T(8,128)} %get-tuple-element.11), kind=kOutput, calls=%fused_computation.23 | convolution fusion | flops 112484416 | bytes 15826944 | tf_op jit(solution)/shard_map/whqk,wqhd->wkhd/dot_general | solution.py:81
  150.0 10.7 %convert_bitcast_fusion = bf16[16,64,24,32]{1,3,2,0:T(8,128)(2,1)} fusion(bf16[16,64,24,32]{1,3,2,0:T(8,128)(2,1)} %copy.23, f32[16,24,64,64]{2,3,1,0:T(8,128)} %get-tuple-element.12, f32[16,24,64]{2,1,0:T(8,128)} %get-tuple-element.11), kind=kOutput, calls=%fused_computation.22 | convolution fusion | flops 104595456 | bytes 9535488 | tf_op jit(solution)/shard_map/whqk,wqhd->wkhd/dot_general | solution.py:71
  160.8 8.1 %convert_bitcast_fusion.3 = bf16[16,64,24,32]{1,3,2,0:T(8,128)(2,1)} fusion(bf16[16,64,24,32]{1,3,2,0:T(8,128)(2,1)S(1)} %bitcast.84, f32[16,24,64,64]{2,3,1,0:T(8,128)} %get-tuple-element.12, f32[16,24,64]{2,1,0:T(8,128)S(1)} %copy-done.26), kind=kOutput, calls=%fused_computation.26 | convolution fusion | flops 104595456 | bytes 9535488 | tf_op jit(solution)/shard_map/whqk,wkhd->wqhd/dot_general | solution.py:53
  168.9 6.9 %copy.20 = bf16[16,64,24,32]{3,2,1,0:T(8,128)(2,1)} copy(bf16[16,64,24,32]{1,3,2,0:T(8,128)(2,1)} %convert_bitcast_fusion.3) | data formatting | bytes 3145728 | tf_op jit(solution)/shard_map/convert_element_type | solution.py:55
  175.8 8.2 %reshape_reshape.19 = bf16[2,8,8,8,768]{4,3,2,1,0:T(8,128)(2,1)} reshape(bf16[16,64,24,32]{3,2,1,0:T(8,128)(2,1)} %copy.20) | data formatting | bytes 3145728 | tf_op jit(solution)/shard_map/reshape;reshape | solution.py:27
  184.1 1.7 copy.21
  185.8 1.1 copy-done.20
  186.9 2.9 fusion.44
  189.8 6.9 %copy.30 = bf16[16,64,24,32]{3,2,1,0:T(8,128)(2,1)} copy(bf16[16,64,24,32]{1,3,2,0:T(8,128)(2,1)} %convert_bitcast_fusion) | data formatting | bytes 3145728 | tf_op jit(solution)/shard_map/convert_element_type | solution.py:73
  196.7 8.2 %concatenate.50 = bf16[2,8,8,8,768]{4,3,2,1,0:T(8,128)(2,1)} reshape(bf16[16,64,24,32]{3,2,1,0:T(8,128)(2,1)} %copy.30) | data formatting | bytes 3145728 | tf_op jit(solution)/shard_map/concatenate | solution.py:85
  204.9 6.9 %copy.27 = bf16[16,64,24,32]{3,2,1,0:T(8,128)(2,1)} copy(bf16[16,64,24,32]{1,3,2,0:T(8,128)(2,1)} %convert_bitcast_fusion.1) | data formatting | bytes 3145728 | tf_op jit(solution)/shard_map/convert_element_type | solution.py:83
  211.8 8.2 %concatenate.49 = bf16[2,8,8,8,768]{4,3,2,1,0:T(8,128)(2,1)} reshape(bf16[16,64,24,32]{3,2,1,0:T(8,128)(2,1)} %copy.27) | data formatting | bytes 3145728 | tf_op jit(solution)/shard_map/concatenate | solution.py:85
  220.0 6.9 %copy.25 = bf16[16,64,24,32]{3,2,1,0:T(8,128)(2,1)} copy(bf16[16,64,24,32]{1,3,2,0:T(8,128)(2,1)} %convert_bitcast_fusion.2) | data formatting | bytes 3145728 | tf_op jit(solution)/shard_map/convert_element_type | solution.py:80
  226.9 8.2 %concatenate.48 = bf16[2,8,8,8,768]{4,3,2,1,0:T(8,128)(2,1)} reshape(bf16[16,64,24,32]{3,2,1,0:T(8,128)(2,1)} %copy.25) | data formatting | bytes 3145728 | tf_op jit(solution)/shard_map/concatenate | solution.py:85
  235.1 2.5 maximum_bitcast_fusion
  238.2 0.9 copy-done.3
  239.6 1.7 copy-done.11
  241.2 6.2 %fusion.43 = f32[768,2304]{1,0:T(8,128)} fusion(bf16[1024,768]{1,0:T(8,128)(2,1)S(1)} %bitcast.101, bf16[1024,2304]{1,0:T(8,128)(2,1)S(1)} %bitcast.90), kind=kOutput, calls=%fused_computation.70 | convolution fusion | flops 3623878656 | bytes 13369344 | tf_op jit(solution)/shard_map/dot_general | solution.py:117
  247.5 3.3 convolution_convert_fusion.2
  251.1 4.1 fusion.39
  255.4 0.9 collective-permute-start.5
  256.3 1.1 multiply_convert_fusion.2
  257.5 6.1 %collective-permute-done.8 = bf16[16,4,768]{2,1,0:T(4,128)(2,1)S(1)} collective-permute-done((bf16[16,4,768]{2,1,0:T(4,128)(2,1)S(1)}, bf16[16,4,768]{2,1,0:T(4,128)(2,1)S(1)}, u32[]{:S(2)}, u32[]{:S(2)}) %collective-permute-start.8) | collective-permute-done | bytes 98336 | tf_op jit(solution)/shard_map/ppermute | solution.py:16
  263.8 3.3 collective-permute-done.5
  267.1 1.9 add_convert_fusion.1
  269.0 12.7 %collective-permute-done.9 = bf16[4,64,768]{2,1,0:T(8,128)(2,1)S(1)} collective-permute-done((bf16[4,64,768]{2,1,0:T(8,128)(2,1)S(1)}, bf16[4,64,768]{2,1,0:T(8,128)(2,1)S(1)}, u32[]{:S(2)}, u32[]{:S(2)}) %collective-permute-start.9) | collective-permute-done | bytes 393248 | tf_op jit(solution)/shard_map/ppermute | solution.py:16
  281.6 1.8 add_convert_fusion
  283.5 135.1 %all-reduce.3.cloned.1.call-done = (f32[768,2304]{1,0:T(8,128)}, f32[768,768]{1,0:T(8,128)}) async-done(((f32[768,2304]{1,0:T(8,128)}, f32[768,768]{1,0:T(8,128)}), (f32[768,2304]{1,0:T(8,128)}, f32[768,768]{1,0:T(8,128)})) %all-reduce.3.cloned.1.call-update) | async-done | bytes 9437200 | tf_op jit(solution)/shard_map/psum | solution.py:158
  418.6 6.6 %copy.42 = f32[768,2304]{1,0:T(8,128)} copy(f32[768,2304]{1,0:T(8,128)} %get-tuple-element.18) | data formatting | bytes 14155776
  425.2 1.4 copy.43
  (82 shorter events, 7.6 us)
Async XLA Ops:
  7.2 48.3 %copy-start = (bf16[768,2304]{1,0:T(8,128)(2,1)S(1)}, bf16[768,2304]{1,0:T(8,128)(2,1)}, u32[]{:S(2)}) copy-start(bf16[768,2304]{1,0:T(8,128)(2,1)} %param.8) | copy-start | bytes 10616836
  7.2 411.4 %all-reduce.3.cloned.1.call-start = ((), (), s32[]{:S(2)}) async-start(), calls=%async_computation | async-start | bytes 18874368 | tf_op jit(solution)/shard_map/psum | solution.py:158
  7.2 13.0 %copy-start.9 = (bf16[16,64,768]{2,1,0:T(8,128)(2,1)S(1)}, bf16[16,64,768]{2,1,0:T(8,128)(2,1)}, u32[]{:S(2)}) copy-start(bf16[16,64,768]{2,1,0:T(8,128)(2,1)} %param.7) | copy-start | bytes 4718596
  8.1 13.2 %collective-permute-start.2 = (bf16[4,64]{1,0:T(4,128)(2,1)S(1)}, bf16[4,64]{1,0:T(4,128)(2,1)S(1)}, u32[]{:S(2)}, u32[]{:S(2)}) collective-permute-start(bf16[4,64]{1,0:T(4,128)(2,1)S(1)} %slice.99), channel_id=1, source_target_pairs={{1,0},{2,1},{3,2},{4,3},{5,4},{6,5},{7,6},{0,7},{9,8},{10,9},{11,1... | collective-permute-start | bytes 1544 | tf_op jit(solution)/shard_map/ppermute | solution.py:16
  14.5 21.3 %collective-permute-start.6 = (bf16[4,64,768]{2,1,0:T(8,128)(2,1)}, bf16[4,64,768]{2,1,0:T(8,128)(2,1)}, u32[]{:S(2)}, u32[]{:S(2)}) collective-permute-start(bf16[4,64,768]{2,1,0:T(8,128)(2,1)} %slice.88), channel_id=1, source_target_pairs={{1,0},{2,1},{3,2},{4,3},{5,4},{6,5},{7,6},{0,7},{9,8},{10,9},{11,1... | collective-permute-start | bytes 1179656 | tf_op jit(solution)/shard_map/ppermute | solution.py:16
  16.9 16.0 %collective-permute-start = (bf16[4,64,768]{2,1,0:T(8,128)(2,1)}, bf16[4,64,768]{2,1,0:T(8,128)(2,1)}, u32[]{:S(2)}, u32[]{:S(2)}) collective-permute-start(bf16[4,64,768]{2,1,0:T(8,128)(2,1)} %slice.73), channel_id=1, source_target_pairs={{1,0},{2,1},{3,2},{4,3},{5,4},{6,5},{7,6},{0,7},{9,8},{10,9},{11,1... | collective-permute-start | bytes 1179656 | tf_op jit(solution)/shard_map/ppermute | solution.py:16
  21.3 4.4 %collective-permute-start.3 = (bf16[16,4]{1,0:T(8,128)(2,1)S(1)}, bf16[16,4]{1,0:T(8,128)(2,1)S(1)}, u32[]{:S(2)}, u32[]{:S(2)}) collective-permute-start(bf16[16,4]{1,0:T(8,128)(2,1)S(1)} %pad_maximum_fusion.8), channel_id=1, source_target_pairs={{8,0},{16,8},{24,16},{32,24},{40,32},{48,40},{56,48},{64,56},{72,6... | collective-permute-start | bytes 392 | tf_op jit(solution)/shard_map/ppermute | solution.py:16
  28.6 13.1 %copy-start.7 = (bf16[12,64,768]{2,1,0:T(8,128)(2,1)S(1)}, bf16[12,64,768]{2,1,0:T(8,128)(2,1)}, u32[]{:S(2)}) copy-start(bf16[12,64,768]{2,1,0:T(8,128)(2,1)} %slice.72) | copy-start | bytes 3538948
  30.2 12.9 %copy-start.6 = (bf16[12,64,768]{2,1,0:T(8,128)(2,1)S(1)}, bf16[12,64,768]{2,1,0:T(8,128)(2,1)}, u32[]{:S(2)}) copy-start(bf16[12,64,768]{2,1,0:T(8,128)(2,1)} %slice.87) | copy-start | bytes 3538948
  33.9 12.1 %collective-permute-start.1 = (bf16[16,4,768]{2,1,0:T(4,128)(2,1)S(1)}, bf16[16,4,768]{2,1,0:T(4,128)(2,1)S(1)}, u32[]{:S(2)}, u32[]{:S(2)}) collective-permute-start(bf16[16,4,768]{2,1,0:T(4,128)(2,1)S(1)} %pad_maximum_fusion.7), channel_id=1, source_target_pairs={{8,0},{16,8},{24,16},{32,24},{40,32},{48,40},{56,48},{64,56},{72,6... | collective-permute-start | bytes 294920 | tf_op jit(solution)/shard_map/ppermute | solution.py:16
  37.5 11.2 %collective-permute-start.7 = (bf16[16,4,768]{2,1,0:T(4,128)(2,1)}, bf16[16,4,768]{2,1,0:T(4,128)(2,1)}, u32[]{:S(2)}, u32[]{:S(2)}) collective-permute-start(bf16[16,4,768]{2,1,0:T(4,128)(2,1)} %pad_maximum_fusion.6), channel_id=1, source_target_pairs={{8,0},{16,8},{24,16},{32,24},{40,32},{48,40},{56,48},{64,56},{72,6... | collective-permute-start | bytes 294920 | tf_op jit(solution)/shard_map/ppermute | solution.py:16
  43.2 4.1 copy-start.1
  46.0 0.6 copy-start.13
  48.6 2.9 copy-start.25
  50.3 1.2 copy-start.18
  53.0 2.0 copy-start.2
  53.0 2.0 copy-start.14
  53.0 2.0 copy-start.21
  53.0 2.0 copy-start.23
  150.0 10.8 %copy-start.5 = (bf16[16,64,768]{1,2,0:T(8,128)(2,1)S(1)}, bf16[16,64,768]{1,2,0:T(8,128)(2,1)}, u32[]{:S(2)}) copy-start(bf16[16,64,768]{1,2,0:T(8,128)(2,1)} %copy.15) | copy-start | bytes 4718596
  150.0 10.8 %copy-start.26 = (f32[16,24,64]{2,1,0:T(8,128)S(1)}, f32[16,24,64]{2,1,0:T(8,128)}, u32[]{:S(2)}) copy-start(f32[16,24,64]{2,1,0:T(8,128)} %get-tuple-element.11) | copy-start | bytes 294916
  184.1 2.8 copy-start.19
  185.7 1.1 copy-start.20
  237.7 1.4 copy-start.3
  237.7 1.4 copy-start.15
  239.1 2.2 copy-start.11
  247.5 3.5 copy-start.4
  247.5 3.6 copy-start.12
  247.5 3.6 copy-start.16
  247.5 3.6 copy-start.22
  247.5 3.6 copy-start.24
  250.9 4.4 %collective-permute-start.4 = (bf16[16,4,768]{2,1,0:T(4,128)(2,1)S(1)}, bf16[16,4,768]{2,1,0:T(4,128)(2,1)S(1)}, u32[]{:S(2)}, u32[]{:S(2)}) collective-permute-start(bf16[16,4,768]{2,1,0:T(4,128)(2,1)S(1)} %slice.104), channel_id=1, source_target_pairs={{120,0},{0,8},{8,16},{16,24},{24,32},{32,40},{40,48},{48,56},{56,6... | collective-permute-start | bytes 294920 | tf_op jit(solution)/shard_map/ppermute | solution.py:16
  255.4 11.7 %collective-permute-start.5 = (bf16[4,64,768]{2,1,0:T(8,128)(2,1)S(1)}, bf16[4,64,768]{2,1,0:T(8,128)(2,1)S(1)}, u32[]{:S(2)}, u32[]{:S(2)}) collective-permute-start(bf16[4,64,768]{2,1,0:T(8,128)(2,1)S(1)} %pad_maximum_fusion.5), channel_id=1, source_target_pairs={{7,0},{0,1},{1,2},{2,3},{3,4},{4,5},{5,6},{6,7},{15,8},{8,9},{9,10... | collective-permute-start | bytes 1179656 | tf_op jit(solution)/shard_map/ppermute | solution.py:16
  256.3 10.8 %copy-start.8 = (bf16[16,64,768]{2,1,0:T(8,128)(2,1)S(1)}, bf16[16,64,768]{2,1,0:T(8,128)(2,1)}, u32[]{:S(2)}) copy-start(bf16[16,64,768]{2,1,0:T(8,128)(2,1)} %param.5) | copy-start | bytes 4718596
  257.4 6.2 %collective-permute-start.8 = (bf16[16,4,768]{2,1,0:T(4,128)(2,1)S(1)}, bf16[16,4,768]{2,1,0:T(4,128)(2,1)S(1)}, u32[]{:S(2)}, u32[]{:S(2)}) collective-permute-start(bf16[16,4,768]{2,1,0:T(4,128)(2,1)S(1)} %slice.108), channel_id=1, source_target_pairs={{120,0},{0,8},{8,16},{16,24},{24,32},{32,40},{40,48},{48,56},{56,6... | collective-permute-start | bytes 294920 | tf_op jit(solution)/shard_map/ppermute | solution.py:16
  263.6 18.0 %copy-start.10 = (bf16[16,64,768]{2,1,0:T(8,128)(2,1)S(1)}, bf16[16,64,768]{2,1,0:T(8,128)(2,1)}, u32[]{:S(2)}) copy-start(bf16[16,64,768]{2,1,0:T(8,128)(2,1)} %param.7) | copy-start | bytes 4718596
  263.8 17.9 %collective-permute-start.9 = (bf16[4,64,768]{2,1,0:T(8,128)(2,1)S(1)}, bf16[4,64,768]{2,1,0:T(8,128)(2,1)S(1)}, u32[]{:S(2)}, u32[]{:S(2)}) collective-permute-start(bf16[4,64,768]{2,1,0:T(8,128)(2,1)S(1)} %pad_maximum_fusion.4), channel_id=1, source_target_pairs={{7,0},{0,1},{1,2},{2,3},{3,4},{4,5},{5,6},{6,7},{15,8},{8,9},{9,10... | collective-permute-start | bytes 1179656 | tf_op jit(solution)/shard_map/ppermute | solution.py:16
  418.6 6.6 %copy-start.17 = (f32[768,768]{1,0:T(8,128)S(1)}, f32[768,768]{1,0:T(8,128)}, u32[]{:S(2)}) copy-start(f32[768,768]{1,0:T(8,128)} %get-tuple-element.19) | copy-start | bytes 7077892
Sparse Core Ops, SparseCore 0:
  247.6 170.9 all-reduce.2
where the time goes:
time: 441 us; the launch traced here: 434 us
  waiting for transfers between devices  163 us (37%)
  local copies, waits for them, and re-layouts  119 us (27%)
  matrix products  101 us (23%)
  other arithmetic  21.9 us (5%)
  between operations  14.7 us (3%)
  starting transfers between devices  14.5 us (3%)
    psum x1, waiting for transfers between devices, local(): grad_wqkv, grad_wout = lax.psum((part_qkv, part_out), ('gx', 'gy'))  135 us
    ppermute x10, waiting for transfers between devices, shifted_2(): return lax.ppermute(block, axis, route)  27.6 us
    concatenate x3, local copies, waits for them, and re-layouts, attend_back(): jnp.concatenate([grad_query.reshape(shape_out), grad_key.reshape(shape_ou...  24.6 us
    dot_general x1, matrix products, attend_back(): jnp.einsum('whqk,wqhd->wkhd', score_half, queries, preferred_element_type...  20 us
    dot_general x1, matrix products, attend_back(): jnp.einsum('whqk,wkhd->wqhd', score_half, keys_part, preferred_element_ty...  19.8 us
    another operation x2, local copies, waits for them, and re-layouts, split_heads(): return tensor.reshape(tensor.shape[0], tensor.shape[1], HEADS, -1)  15.2 us
    ppermute x10, starting transfers between devices, shifted_2(): return lax.ppermute(block, axis, route)  14.5 us
    unnamed x56, local copies, waits for them, and re-layouts  14 us
  transfers between devices with their start and end apart: 11, of which 6 were waited for; matrix products, arithmetic and copies ran while one was open for 8% of the time, Pallas kernels for 0%

commit v1 on v0

--- a/solution.py
+++ b/solution.py
@@ -155,7 +155,7 @@
     from_above = shifted_2((wide_attn[bottom:], wide_grad[bottom:]), "gy", 1)
     attn_tile = jnp.concatenate([from_above[0], wide_attn[:bottom]], 0)
     grad_tile = jnp.concatenate([from_above[1], wide_grad[:bottom]], 0)
-    grad_wqkv, grad_wout = lax.psum((part_qkv, part_out), ("gx", "gy"))
+    grad_wqkv, grad_wout = lax.psum(lax.psum((part_qkv, part_out), "gy"), "gx")
     block_out = (slide_tokens.astype(jnp.float32) + attn_tile.astype(jnp.float32)).astype(
         jnp.bfloat16
     )

time: 441 us -> 648 us (1.47)
  waiting for transfers between devices: 163 us -> 365 us
    psum x1 -> x2, waiting for transfers between devices: 135 us -> 330 us  [local(): grad_wqkv, grad_wout = lax.psum(lax.psum((part_qkv, part_out), 'gy'), 'gx')]
    ppermute x10, waiting for transfers between devices: 27.6 us -> 35.3 us  [shifted_2(): return lax.ppermute(block, axis, route)]
    unnamed x56 -> x54, local copies, waits for them, and re-layouts: 14 us -> 13.9 us
  transfers between devices with their start and end apart: 11 -> 12, of which waited for: 6 -> 7; matrix products, arithmetic and copies ran while one was open for 8% -> 6% of each run, Pallas kernels for 0% -> 0%
where the time goes in v1:
time: 648 us; the launch traced here: 640 us
  waiting for transfers between devices  365 us (56%)
  local copies, waits for them, and re-layouts  119 us (18%)
  matrix products  103 us (16%)
  other arithmetic  21.9 us (3%)
  starting transfers between devices  16.3 us (3%)
  between operations  14.7 us (2%)
    psum x2, waiting for transfers between devices, local(): grad_wqkv, grad_wout = lax.psum(lax.psum((part_qkv, part_out), 'gy'), 'gx')  330 us
    ppermute x10, waiting for transfers between devices, shifted_2(): return lax.ppermute(block, axis, route)  35.3 us
    concatenate x3, local copies, waits for them, and re-layouts, attend_back(): jnp.concatenate([grad_query.reshape(shape_out), grad_key.reshape(shape_ou...  24.6 us
    dot_general x1, matrix products, attend_back(): jnp.einsum('whqk,wqhd->wkhd', score_half, queries, preferred_element_type...  20.1 us
    dot_general x1, matrix products, attend_back(): jnp.einsum('whqk,wkhd->wqhd', score_half, keys_part, preferred_element_ty...  19.8 us
    ppermute x10, starting transfers between devices, shifted_2(): return lax.ppermute(block, axis, route)  16.3 us
    another operation x2, local copies, waits for them, and re-layouts, split_heads(): return tensor.reshape(tensor.shape[0], tensor.shape[1], HEADS, -1)  15.3 us
    unnamed x54, local copies, waits for them, and re-layouts  13.9 us
  transfers between devices with their start and end apart: 12, of which 7 were waited for; matrix products, arithmetic and copies ran while one was open for 6% of the time, Pallas kernels for 0%

profile of v1, /device:TPU:1, one launch (start us, length us, event | category | flops | bytes accessed | tf_op | source)
XLA Modules:
  0.0 639.5 jit_solution(6700651859739096700)
XLA Ops:
  7.2 0.9 convert_element_type.101
  8.1 4.7 collective-permute-start.2
  12.8 1.8 slice.88
  15.2 1.8 slice.73
  17.8 2.4 slice.72
  20.2 1.1 slice.87
  21.3 1.5 collective-permute-start.3
  22.9 2.8 collective-permute-done.3
  26.4 0.8 gt.22
  27.8 0.8 gt.24
  28.6 1.7 broadcast_or_fusion
  30.3 2.7 collective-permute-done
  32.9 1.0 pad_maximum_fusion.7
  33.9 1.9 collective-permute-start.1
  35.8 1.6 pad_maximum_fusion.6
  37.5 4.3 collective-permute-start.7
  41.7 1.4 slice_maximum_fusion.1
  43.2 2.8 slice_maximum_fusion
  48.6 1.7 pad_maximum_fusion.3
  50.3 1.2 copy-done.18
  51.6 1.4 convolution_convert_fusion.1
  53.0 1.3 copy.38
  55.5 4.5 convolution_convert_fusion
  60.5 2.3 fusion.40
  62.8 4.2 copy.18
  66.9 4.1 copy.17
  71.1 4.2 copy.15
  75.2 8.2 %reshape_reshape.22 = bf16[16,64,24,32]{3,2,1,0:T(8,128)(2,1)} reshape(bf16[2,8,8,8,768]{4,3,2,1,0:T(8,128)(2,1)} %bitcast.88) | data formatting | bytes 3145728 | tf_op jit(solution)/shard_map/reshape;reshape | solution.py:32
  83.4 7.1 %copy.23 = bf16[16,64,24,32]{1,3,2,0:T(8,128)(2,1)} copy(bf16[16,64,24,32]{3,2,1,0:T(8,128)(2,1)} %reshape_reshape.22) | data formatting | bytes 3145728 | tf_op jit(solution)/shard_map/reshape;reshape | solution.py:32
  90.5 9.2 %fusion.42 = f32[16,24,64,64]{2,3,1,0:T(8,128)} fusion(bf16[16,64,24,32]{1,3,2,0:T(8,128)(2,1)} %copy.23, bf16[16,64,24,32]{1,3,2,0:T(8,128)(2,1)} %bitcast.83), kind=kOutput, calls=%fused_computation.69 | convolution fusion | flops 100663296 | bytes 9437184 | tf_op jit(solution)/shard_map/wqhd,wkhd->whqk/dot_general | solution.py:67
  99.7 10.5 %fusion.41 = (f32[16,24,64]{2,1,0:T(8,128)}, f32[16,24,64,64]{2,3,1,0:T(8,128)}) fusion(pred[16,64,64]{1,2,0:T(8,128)(4,1)} %broadcast_or_fusion, bf16[16,64,24,32]{1,3,2,0:T(8,128)(2,1)} %bitcast.95, bf16[16,64,24,32]{1,3,2,0:T(8,128)(2,1)} %bitcast.93), kind=kOutput, calls=%fused_computation.68 | convolution fusion | flops 106954816 | bytes 9601024 | tf_op jit(solution)/shard_map/sub | solution.py:50
  110.2 19.8 %convert_bitcast_fusion.2 = bf16[16,64,24,32]{1,3,2,0:T(8,128)(2,1)} fusion(bf16[16,64,24,32]{1,3,2,0:T(8,128)(2,1)} %bitcast.94, f32[16,24,64,64]{2,3,1,0:T(8,128)} %fusion.42, f32[16,24,64,64]{2,3,1,0:T(8,128)} %get-tuple-element.14, f32[16,24,64]{2,1,0:T(8,128)} %get-tuple-element.13), kind=kOutput, calls=%fused_computation.24 | convolution fusion | flops 112484416 | bytes 15826944 | tf_op jit(solution)/shard_map/whqk,wkhd->wqhd/dot_general | solution.py:78
  129.9 20.1 %convert_bitcast_fusion.1 = bf16[16,64,24,32]{1,3,2,0:T(8,128)(2,1)} fusion(bf16[16,64,24,32]{1,3,2,0:T(8,128)(2,1)} %bitcast.96, f32[16,24,64,64]{2,3,1,0:T(8,128)} %fusion.42, f32[16,24,64,64]{2,3,1,0:T(8,128)} %get-tuple-element.14, f32[16,24,64]{2,1,0:T(8,128)} %get-tuple-element.13), kind=kOutput, calls=%fused_computation.23 | convolution fusion | flops 112484416 | bytes 15826944 | tf_op jit(solution)/shard_map/whqk,wqhd->wkhd/dot_general | solution.py:81
  150.0 10.7 %convert_bitcast_fusion = bf16[16,64,24,32]{1,3,2,0:T(8,128)(2,1)} fusion(bf16[16,64,24,32]{1,3,2,0:T(8,128)(2,1)} %copy.23, f32[16,24,64,64]{2,3,1,0:T(8,128)} %get-tuple-element.14, f32[16,24,64]{2,1,0:T(8,128)} %get-tuple-element.13), kind=kOutput, calls=%fused_computation.22 | convolution fusion | flops 104595456 | bytes 9535488 | tf_op jit(solution)/shard_map/whqk,wqhd->wkhd/dot_general | solution.py:71
  160.8 8.2 %convert_bitcast_fusion.3 = bf16[16,64,24,32]{1,3,2,0:T(8,128)(2,1)} fusion(bf16[16,64,24,32]{1,3,2,0:T(8,128)(2,1)S(1)} %bitcast.84, f32[16,24,64,64]{2,3,1,0:T(8,128)} %get-tuple-element.14, f32[16,24,64]{2,1,0:T(8,128)S(1)} %copy-done.25), kind=kOutput, calls=%fused_computation.26 | convolution fusion | flops 104595456 | bytes 9535488 | tf_op jit(solution)/shard_map/whqk,wkhd->wqhd/dot_general | solution.py:53
  168.9 6.9 %copy.20 = bf16[16,64,24,32]{3,2,1,0:T(8,128)(2,1)} copy(bf16[16,64,24,32]{1,3,2,0:T(8,128)(2,1)} %convert_bitcast_fusion.3) | data formatting | bytes 3145728 | tf_op jit(solution)/shard_map/convert_element_type | solution.py:55
  175.8 8.2 %reshape_reshape.19 = bf16[2,8,8,8,768]{4,3,2,1,0:T(8,128)(2,1)} reshape(bf16[16,64,24,32]{3,2,1,0:T(8,128)(2,1)} %copy.20) | data formatting | bytes 3145728 | tf_op jit(solution)/shard_map/reshape;reshape | solution.py:27
  184.1 1.7 copy.21
  185.8 1.1 copy-done.17
  186.9 2.9 fusion.44
  189.8 6.9 %copy.30 = bf16[16,64,24,32]{3,2,1,0:T(8,128)(2,1)} copy(bf16[16,64,24,32]{1,3,2,0:T(8,128)(2,1)} %convert_bitcast_fusion) | data formatting | bytes 3145728 | tf_op jit(solution)/shard_map/convert_element_type | solution.py:73
  196.7 8.2 %concatenate.50 = bf16[2,8,8,8,768]{4,3,2,1,0:T(8,128)(2,1)} reshape(bf16[16,64,24,32]{3,2,1,0:T(8,128)(2,1)} %copy.30) | data formatting | bytes 3145728 | tf_op jit(solution)/shard_map/concatenate | solution.py:85
  204.9 6.9 %copy.27 = bf16[16,64,24,32]{3,2,1,0:T(8,128)(2,1)} copy(bf16[16,64,24,32]{1,3,2,0:T(8,128)(2,1)} %convert_bitcast_fusion.1) | data formatting | bytes 3145728 | tf_op jit(solution)/shard_map/convert_element_type | solution.py:83
  211.8 8.2 %concatenate.49 = bf16[2,8,8,8,768]{4,3,2,1,0:T(8,128)(2,1)} reshape(bf16[16,64,24,32]{3,2,1,0:T(8,128)(2,1)} %copy.27) | data formatting | bytes 3145728 | tf_op jit(solution)/shard_map/concatenate | solution.py:85
  220.0 6.9 %copy.25 = bf16[16,64,24,32]{3,2,1,0:T(8,128)(2,1)} copy(bf16[16,64,24,32]{1,3,2,0:T(8,128)(2,1)} %convert_bitcast_fusion.2) | data formatting | bytes 3145728 | tf_op jit(solution)/shard_map/convert_element_type | solution.py:80
  226.9 8.2 %concatenate.48 = bf16[2,8,8,8,768]{4,3,2,1,0:T(8,128)(2,1)} reshape(bf16[16,64,24,32]{3,2,1,0:T(8,128)(2,1)} %copy.25) | data formatting | bytes 3145728 | tf_op jit(solution)/shard_map/concatenate | solution.py:85
  235.2 2.5 maximum_bitcast_fusion
  238.2 0.9 copy-done.3
  239.6 1.6 copy-done.11
  241.2 6.2 fusion.43
  247.5 201.6 %all-reduce.7.cloned.1.call-done = (f32[768,2304]{1,0:T(8,128)}, f32[768,768]{1,0:T(8,128)}) async-done(((f32[768,2304]{1,0:T(8,128)}, f32[768,768]{1,0:T(8,128)}), (f32[768,2304]{1,0:T(8,128)}, f32[768,768]{1,0:T(8,128)})) %all-reduce.7.cloned.1.call-update) | async-done | bytes 9437200 | tf_op jit(solution)/shard_map/psum | solution.py:158
  449.2 3.3 convolution_convert_fusion.2
  452.5 1.8 collective-permute-start.4
  454.4 6.1 fusion.39
  460.7 1.1 multiply_convert_fusion.2
  462.0 2.0 collective-permute-done.8
  464.2 0.9 collective-permute-start.9
  465.1 15.2 %collective-permute-done.5 = bf16[4,64,768]{2,1,0:T(8,128)(2,1)S(1)} collective-permute-done((bf16[4,64,768]{2,1,0:T(8,128)(2,1)S(1)}, bf16[4,64,768]{2,1,0:T(8,128)(2,1)S(1)}, u32[]{:S(2)}, u32[]{:S(2)}) %collective-permute-start.5) | collective-permute-done | bytes 393248 | tf_op jit(solution)/shard_map/ppermute | solution.py:16
  480.3 1.9 add_convert_fusion.1
  482.2 12.5 %collective-permute-done.9 = bf16[4,64,768]{2,1,0:T(8,128)(2,1)S(1)} collective-permute-done((bf16[4,64,768]{2,1,0:T(8,128)(2,1)S(1)}, bf16[4,64,768]{2,1,0:T(8,128)(2,1)S(1)}, u32[]{:S(2)}, u32[]{:S(2)}) %collective-permute-start.9) | collective-permute-done | bytes 393248 | tf_op jit(solution)/shard_map/ppermute | solution.py:16
  494.7 1.9 add_convert_fusion
  496.6 127.9 %all-reduce.5.cloned.1.call-done = (f32[768,2304]{1,0:T(8,128)}, f32[768,768]{1,0:T(8,128)}) async-done(((f32[768,2304]{1,0:T(8,128)}, f32[768,768]{1,0:T(8,128)}), (f32[768,2304]{1,0:T(8,128)}, f32[768,768]{1,0:T(8,128)})) %all-reduce.5.cloned.1.call-update) | async-done | bytes 9437200 | tf_op jit(solution)/shard_map/psum | solution.py:158
  624.5 6.6 %copy.44 = f32[768,2304]{1,0:T(8,128)} copy(f32[768,2304]{1,0:T(8,128)} %get-tuple-element.20) | data formatting | bytes 14155776
  631.1 1.4 copy.45
  (83 shorter events, 8.8 us)
Async XLA Ops:
  7.2 48.3 %copy-start = (bf16[768,2304]{1,0:T(8,128)(2,1)S(1)}, bf16[768,2304]{1,0:T(8,128)(2,1)}, u32[]{:S(2)}) copy-start(bf16[768,2304]{1,0:T(8,128)(2,1)} %param.8) | copy-start | bytes 10616836
  7.2 442.0 %all-reduce.7.cloned.1.call-start = ((), (), s32[]{:S(2)}) async-start(), calls=%async_computation.1 | async-start | bytes 18874368 | tf_op jit(solution)/shard_map/psum | solution.py:158
  7.2 13.0 %copy-start.9 = (bf16[16,64,768]{2,1,0:T(8,128)(2,1)S(1)}, bf16[16,64,768]{2,1,0:T(8,128)(2,1)}, u32[]{:S(2)}) copy-start(bf16[16,64,768]{2,1,0:T(8,128)(2,1)} %param.7) | copy-start | bytes 4718596
  8.1 13.2 %collective-permute-start.2 = (bf16[4,64]{1,0:T(4,128)(2,1)S(1)}, bf16[4,64]{1,0:T(4,128)(2,1)S(1)}, u32[]{:S(2)}, u32[]{:S(2)}) collective-permute-start(bf16[4,64]{1,0:T(4,128)(2,1)S(1)} %slice.99), channel_id=1, source_target_pairs={{1,0},{2,1},{3,2},{4,3},{5,4},{6,5},{7,6},{0,7},{9,8},{10,9},{11,1... | collective-permute-start | bytes 1544 | tf_op jit(solution)/shard_map/ppermute | solution.py:16
  14.5 21.3 %collective-permute-start.6 = (bf16[4,64,768]{2,1,0:T(8,128)(2,1)}, bf16[4,64,768]{2,1,0:T(8,128)(2,1)}, u32[]{:S(2)}, u32[]{:S(2)}) collective-permute-start(bf16[4,64,768]{2,1,0:T(8,128)(2,1)} %slice.88), channel_id=1, source_target_pairs={{1,0},{2,1},{3,2},{4,3},{5,4},{6,5},{7,6},{0,7},{9,8},{10,9},{11,1... | collective-permute-start | bytes 1179656 | tf_op jit(solution)/shard_map/ppermute | solution.py:16
  16.9 16.0 %collective-permute-start = (bf16[4,64,768]{2,1,0:T(8,128)(2,1)}, bf16[4,64,768]{2,1,0:T(8,128)(2,1)}, u32[]{:S(2)}, u32[]{:S(2)}) collective-permute-start(bf16[4,64,768]{2,1,0:T(8,128)(2,1)} %slice.73), channel_id=1, source_target_pairs={{1,0},{2,1},{3,2},{4,3},{5,4},{6,5},{7,6},{0,7},{9,8},{10,9},{11,1... | collective-permute-start | bytes 1179656 | tf_op jit(solution)/shard_map/ppermute | solution.py:16
  21.3 4.4 collective-permute-start.3
  28.6 13.1 %copy-start.7 = (bf16[12,64,768]{2,1,0:T(8,128)(2,1)S(1)}, bf16[12,64,768]{2,1,0:T(8,128)(2,1)}, u32[]{:S(2)}) copy-start(bf16[12,64,768]{2,1,0:T(8,128)(2,1)} %slice.72) | copy-start | bytes 3538948
  30.3 12.9 %copy-start.6 = (bf16[12,64,768]{2,1,0:T(8,128)(2,1)S(1)}, bf16[12,64,768]{2,1,0:T(8,128)(2,1)}, u32[]{:S(2)}) copy-start(bf16[12,64,768]{2,1,0:T(8,128)(2,1)} %slice.87) | copy-start | bytes 3538948
  33.9 12.1 %collective-permute-start.1 = (bf16[16,4,768]{2,1,0:T(4,128)(2,1)S(1)}, bf16[16,4,768]{2,1,0:T(4,128)(2,1)S(1)}, u32[]{:S(2)}, u32[]{:S(2)}) collective-permute-start(bf16[16,4,768]{2,1,0:T(4,128)(2,1)S(1)} %pad_maximum_fusion.7), channel_id=1, source_target_pairs={{8,0},{16,8},{24,16},{32,24},{40,32},{48,40},{56,48},{64,56},{72,6... | collective-permute-start | bytes 294920 | tf_op jit(solution)/shard_map/ppermute | solution.py:16
  37.5 11.2 %collective-permute-start.7 = (bf16[16,4,768]{2,1,0:T(4,128)(2,1)}, bf16[16,4,768]{2,1,0:T(4,128)(2,1)}, u32[]{:S(2)}, u32[]{:S(2)}) collective-permute-start(bf16[16,4,768]{2,1,0:T(4,128)(2,1)} %pad_maximum_fusion.6), channel_id=1, source_target_pairs={{8,0},{16,8},{24,16},{32,24},{40,32},{48,40},{56,48},{64,56},{72,6... | collective-permute-start | bytes 294920 | tf_op jit(solution)/shard_map/ppermute | solution.py:16
  43.2 4.1 copy-start.1
  46.0 0.6 copy-start.12
  48.6 2.9 copy-start.24
  50.3 1.2 copy-start.18
  53.0 2.0 copy-start.2
  53.0 2.0 copy-start.13
  53.0 2.0 copy-start.20
  53.0 2.0 copy-start.22
  150.0 10.7 %copy-start.5 = (bf16[16,64,768]{1,2,0:T(8,128)(2,1)S(1)}, bf16[16,64,768]{1,2,0:T(8,128)(2,1)}, u32[]{:S(2)}) copy-start(bf16[16,64,768]{1,2,0:T(8,128)(2,1)} %copy.15) | copy-start | bytes 4718596
  150.0 10.7 %copy-start.25 = (f32[16,24,64]{2,1,0:T(8,128)S(1)}, f32[16,24,64]{2,1,0:T(8,128)}, u32[]{:S(2)}) copy-start(f32[16,24,64]{2,1,0:T(8,128)} %get-tuple-element.13) | copy-start | bytes 294916
  184.1 2.8 copy-start.19
  185.7 1.1 copy-start.17
  237.7 1.4 copy-start.3
  237.7 1.4 copy-start.14
  239.1 2.1 copy-start.11
  247.4 377.0 %all-reduce.5.cloned.1.call-start = ((), (), s32[]{:S(2)}) async-start(), calls=%async_computation | async-start | bytes 18874368 | tf_op jit(solution)/shard_map/psum | solution.py:158
  449.2 5.2 copy-start.4
  449.2 5.2 copy-start.15
  449.2 5.2 copy-start.21
  449.2 5.2 copy-start.23
  452.5 8.0 %collective-permute-start.4 = (bf16[16,4,768]{2,1,0:T(4,128)(2,1)S(1)}, bf16[16,4,768]{2,1,0:T(4,128)(2,1)S(1)}, u32[]{:S(2)}, u32[]{:S(2)}) collective-permute-start(bf16[16,4,768]{2,1,0:T(4,128)(2,1)S(1)} %slice.104), channel_id=1, source_target_pairs={{120,0},{0,8},{8,16},{16,24},{24,32},{32,40},{40,48},{48,56},{56,6... | collective-permute-start | bytes 294920 | tf_op jit(solution)/shard_map/ppermute | solution.py:16
  460.6 19.7 %collective-permute-start.5 = (bf16[4,64,768]{2,1,0:T(8,128)(2,1)S(1)}, bf16[4,64,768]{2,1,0:T(8,128)(2,1)S(1)}, u32[]{:S(2)}, u32[]{:S(2)}) collective-permute-start(bf16[4,64,768]{2,1,0:T(8,128)(2,1)S(1)} %pad_maximum_fusion.5), channel_id=1, source_target_pairs={{7,0},{0,1},{1,2},{2,3},{3,4},{4,5},{5,6},{6,7},{15,8},{8,9},{9,10... | collective-permute-start | bytes 1179656 | tf_op jit(solution)/shard_map/ppermute | solution.py:16
  460.7 19.6 %copy-start.8 = (bf16[16,64,768]{2,1,0:T(8,128)(2,1)S(1)}, bf16[16,64,768]{2,1,0:T(8,128)(2,1)}, u32[]{:S(2)}) copy-start(bf16[16,64,768]{2,1,0:T(8,128)(2,1)} %param.5) | copy-start | bytes 4718596
  461.9 2.1 collective-permute-start.8
  464.0 30.7 %copy-start.10 = (bf16[16,64,768]{2,1,0:T(8,128)(2,1)S(1)}, bf16[16,64,768]{2,1,0:T(8,128)(2,1)}, u32[]{:S(2)}) copy-start(bf16[16,64,768]{2,1,0:T(8,128)(2,1)} %param.7) | copy-start | bytes 4718596
  464.2 30.5 %collective-permute-start.9 = (bf16[4,64,768]{2,1,0:T(8,128)(2,1)S(1)}, bf16[4,64,768]{2,1,0:T(8,128)(2,1)S(1)}, u32[]{:S(2)}, u32[]{:S(2)}) collective-permute-start(bf16[4,64,768]{2,1,0:T(8,128)(2,1)S(1)} %pad_maximum_fusion.4), channel_id=1, source_target_pairs={{7,0},{0,1},{1,2},{2,3},{3,4},{4,5},{5,6},{6,7},{15,8},{8,9},{9,10... | collective-permute-start | bytes 1179656 | tf_op jit(solution)/shard_map/ppermute | solution.py:16
  624.5 6.6 %copy-start.16 = (f32[768,768]{1,0:T(8,128)S(1)}, f32[768,768]{1,0:T(8,128)}, u32[]{:S(2)}) copy-start(f32[768,768]{1,0:T(8,128)} %get-tuple-element.21) | copy-start | bytes 7077892
Sparse Core Ops, SparseCore 0:
  247.6 201.5 all-reduce.6
  451.7 172.7 all-reduce.4
